TPU v7x, 512 devices: a whole 4x4x16 slice. The times are simulated.
512 devices in a mesh: section: 4 (over x), seq: 16 (over y, z_lo), wide: 8 (over z_hi, core).
Axes of the slice: x: 4, y: 4, z: 16 (z_hi: 4, z_lo: 4; z = z_hi * 4 + z_lo), core: 2. Of those that a mesh axis runs over, the one named last changes fastest.
Arguments:
- q_self: bfloat16 [4, 4096, 5120], P('section', 'seq', 'wide'), may hold values from -6 to 6
- k_self: bfloat16 [4, 4096, 5120], P('section', 'seq', 'wide'), may hold values from -6 to 6
- v_self: bfloat16 [4, 4096, 5120], P('section', 'seq', 'wide'), may hold values from -6 to 6
- gain_q_self: float32 [5120], P('wide'), may hold values from 1.2 to 2.4
- gain_k_self: float32 [5120], P('wide'), may hold values from 1.2 to 2.4
- counts: int32 [4], replicated, may hold values from 1 to 4096, 12288 in all
- q_cross: bfloat16 [4, 4096, 5120], P('section', 'seq', 'wide'), may hold values from -6 to 6
- cap_kv: bfloat16 [2, 4, 512, 5120], P(None, 'section', 'seq', 'wide'), may hold values from -6 to 6
- gain_q_cross: float32 [5120], P('wide'), may hold values from 1.2 to 2.4
- gain_k_cross: float32 [5120], P('wide'), may hold values from 1.2 to 2.4
- cap_len: int32 [4], replicated, may hold values from 1 to 512, 1024 in all
- owner: int32 [4], replicated, may hold values from 0 to 3, each once
Outputs:
- out_self: bfloat16 [4, 4096, 5120], P('section', 'seq', 'wide')
- out_cross: bfloat16 [4, 4096, 5120], P('section', 'seq', 'wide')
Inputs may be any that keep to these rules, and one draw needn't show every extreme that they name: owner is a permutation of the clips.
All inputs are finite; a program needn't handle non-finite values.
Results may differ from a plain program's by a relative error of at most 0.012.
The roundings to bfloat16 on the way count: a program that leaves them out, or rounds other values in their place, can miss the bound.
Values may be sent and summed in bfloat16 or wider, within the bound.
A program may use at most 128 MiB of HBM per device.

v0:
```python
import math

import jax
import jax.numpy as jnp
from jax import lax
from jax.sharding import PartitionSpec as P

D = 5120
HEAD = 128


masked_score = -1e30


def square_sums(values):
    floats = values.astype(jnp.float32)
    return jnp.sum(floats * floats, axis=-1)


def scaled_rows(values, total_squares, gain):
    floats = values.astype(jnp.float32)
    factor = lax.rsqrt(total_squares / D + 1e-06)
    return (floats * factor[:, None] * gain[None, :]).astype(jnp.bfloat16)


def start_state(heads_here, rows):
    running = jnp.full((heads_here, rows), masked_score, jnp.float32)
    totals = jnp.zeros((heads_here, rows), jnp.float32)
    accum = jnp.zeros((heads_here, rows, HEAD), jnp.float32)
    return (running, totals, accum)


def attend_rows(state, queries, keys, values, limit):
    heads_here = queries.shape[1]
    count_rows = keys.shape[0]
    block_rows = math.gcd(count_rows, 512)
    blocks = count_rows // block_rows
    key_blocks = keys.reshape(blocks, block_rows, heads_here, HEAD)
    value_blocks = values.reshape(blocks, block_rows, heads_here, HEAD)
    factor = 1.0 / math.sqrt(HEAD)

    def one_block(carry, inputs):
        running, totals, accum = carry
        key_block, value_block, number = inputs
        scores = (
            jnp.einsum("qhd,khd->hqk", queries, key_block, preferred_element_type=jnp.float32)
            * factor
        )
        position = number * block_rows + jnp.arange(block_rows, dtype=jnp.int32)
        scores = jnp.where((position < limit)[None, None, :], scores, masked_score)
        newest = jnp.maximum(running, jnp.max(scores, axis=-1))
        rescale = jnp.exp(running - newest)
        weights = jnp.exp(scores - newest[:, :, None])
        totals = totals * rescale + jnp.sum(weights, axis=-1)
        update = jnp.einsum(
            "hqk,khd->hqd",
            weights.astype(jnp.bfloat16),
            value_block,
            preferred_element_type=jnp.float32,
        )
        accum = accum * rescale[:, :, None] + update
        return ((newest, totals, accum), None)

    numbers = jnp.arange(blocks, dtype=jnp.int32)
    state, unused = lax.scan(one_block, state, (key_blocks, value_blocks, numbers))
    return state


def finish(state):
    running, totals, accum = state
    result = accum / totals[:, :, None]
    heads_here, rows, width = result.shape
    return result.transpose(1, 0, 2).reshape(rows, heads_here * width).astype(jnp.bfloat16)[None]


def per_device(
    q_self,
    k_self,
    v_self,
    gain_q_self,
    gain_k_self,
    counts,
    q_cross,
    cap_kv,
    gain_q_cross,
    gain_k_cross,
    cap_len,
    owner,
):
    rows = q_self.shape[1]
    heads_here = q_self.shape[2] // HEAD
    section_index = lax.axis_index("section")
    section_count = lax.axis_size("section")
    latent_count = lax.dynamic_index_in_dim(counts, section_index, 0, keepdims=False)
    totals = lax.psum(
        (square_sums(q_self[0]), square_sums(k_self[0]), square_sums(q_cross[0])), "wide"
    )
    q_hat = scaled_rows(q_self[0], totals[0], gain_q_self).reshape(rows, heads_here, HEAD)
    k_hat = scaled_rows(k_self[0], totals[1], gain_k_self)
    cross_hat = scaled_rows(q_cross[0], totals[2], gain_q_cross).reshape(rows, heads_here, HEAD)
    keys = lax.all_gather(k_hat[None], "seq", axis=1, tiled=True)
    values = lax.all_gather(v_self, "seq", axis=1, tiled=True)
    count_rows = keys.shape[1]
    self_state = attend_rows(
        start_state(heads_here, rows),
        q_hat,
        keys[0].reshape(count_rows, heads_here, HEAD),
        values[0].reshape(count_rows, heads_here, HEAD),
        latent_count,
    )
    out_self = finish(self_state)
    section_numbers = jnp.arange(section_count, dtype=jnp.int32)
    source = jnp.sum(jnp.where(owner == section_index, section_numbers, 0))
    caption_length = lax.dynamic_index_in_dim(cap_len, source, 0, keepdims=False)
    whole = lax.all_gather(cap_kv, "seq", axis=2, tiled=True)
    key_totals = lax.psum(square_sums(whole[0, 0]), "wide")
    own_keys = scaled_rows(whole[0, 0], key_totals, gain_k_cross)
    assembled = jnp.stack([own_keys, whole[1, 0]])[:, None]
    routed = lax.all_gather(assembled, "section", axis=1, tiled=True)
    chosen = lax.dynamic_index_in_dim(routed, source, 1, keepdims=False)
    count_rows = chosen.shape[1]
    cross_state = attend_rows(
        start_state(heads_here, rows),
        cross_hat,
        chosen[0].reshape(count_rows, heads_here, HEAD),
        chosen[1].reshape(count_rows, heads_here, HEAD),
        caption_length,
    )
    out_cross = finish(cross_state)
    return (out_self, out_cross)


def solution(mesh):
    return jax.shard_map(
        per_device,
        mesh=mesh,
        in_specs=(
            P("section", "seq", "wide"),
            P("section", "seq", "wide"),
            P("section", "seq", "wide"),
            P("wide"),
            P("wide"),
            P(),
            P("section", "seq", "wide"),
            P(None, "section", "seq", "wide"),
            P("wide"),
            P("wide"),
            P(),
            P(),
        ),
        out_specs=(P("section", "seq", "wide"), P("section", "seq", "wide")),
        check_vma=False,
    )
```

profile of v0, /device:TPU:1, one launch (start us, length us, event | category | flops | bytes accessed | tf_op | source)
XLA Modules:
  0.0 517.4 jit_solution(16021521661886454871)
XLA Ops:
  8.7 1.1 copy.40
  9.8 1.1 copy.34
  11.2 1.1 fusion.47
  12.3 82.7 %all-gather.10.cloned.1.call-done = bf16[2,1,512,640]{3,2,1,0:T(8,128)(2,1)} async-done(((bf16[2,1,32,640]{3,2,1,0:T(8,128)(2,1)}), bf16[2,1,512,640]{3,2,1,0:T(8,128)(2,1)}) %all-gather.10.cloned.1.call-update) | async-done | bytes 1310736 | tf_op jit(solution)/shard_map/all_gather | solution.py:115
  95.1 1.3 fusion.28
  96.4 27.6 %all-reduce = (f32[256]{0:T(256)S(1)}, f32[256]{0:T(256)S(1)}, f32[512]{0:T(512)S(1)}, f32[256]{0:T(256)S(1)}) all-reduce(f32[256]{0:T(256)S(1)} %fusion.47, f32[256]{0:T(256)S(1)} %multiply_reduce_fusion.1, f32[512]{0:T(512)S(1)} %fusion.28, f32[256]{0:T(256)S(1)} %multiply_reduce_fusion), channel_id=1, replica_groups=mesh['section'=4,'seq'=16,'wide'=8] {'wide'}, use_global_device_ids=true, to_apply=%region_1.2 | all-reduce | flops 1280 | bytes 10240 | tf_op jit(solution)/shard_map/psum | solution.py:95
  124.0 1.1 slice_bitcast_fusion
  125.2 1.4 fusion.27
  126.6 1.3 pad_maximum_fusion
  128.0 0.9 fusion.49
  133.7 98.9 %all-gather.8.cloned.1.call-done = bf16[1,4096,640]{2,1,0:T(8,128)(2,1)} async-done(((bf16[1,256,640]{2,1,0:T(8,128)(2,1)}), bf16[1,4096,640]{2,1,0:T(8,128)(2,1)}) %all-gather.8.cloned.1.call-update) | async-done | bytes 5242896 | tf_op jit(solution)/shard_map/all_gather | solution.py:102
  232.6 12.6 %reshape.180 = bf16[8,512,5,128]{3,2,1,0:T(8,128)(2,1)} reshape(bf16[1,4096,640]{2,1,0:T(8,128)(2,1)} %all-gather.8.cloned.1.call-done) | data formatting | bytes 10485760 | tf_op jit(solution)/shard_map/reshape;reshape;squeeze | solution.py:39
  245.3 7.2 %copy.38 = bf16[8,512,5,128]{3,1,2,0:T(8,128)(2,1)} copy(bf16[8,512,5,128]{3,2,1,0:T(8,128)(2,1)} %reshape.180) | data formatting | bytes 10485760
  252.5 44.5 %all-gather.12.cloned.1.call-done = bf16[2,2048,640]{2,1,0:T(8,128)(2,1)} async-done(((bf16[2,512,640]{2,1,0:T(8,128)(2,1)}), bf16[2,2048,640]{2,1,0:T(8,128)(2,1)}) %all-gather.12.cloned.1.call-update) | async-done | bytes 5242896 | tf_op jit(solution)/shard_map/all_gather | solution.py:119
  297.0 1.4 constant_dynamic-slice_fusion
  299.0 1.0 fusion.22
  300.7 0.8 fusion.44
  301.6 0.9 copy.46
  302.5 125.5 %all-gather.6.cloned.1.call-done = bf16[1,4096,640]{2,1,0:T(8,128)(2,1)} async-done(((bf16[1,256,640]{2,1,0:T(8,128)(2,1)}), bf16[1,4096,640]{2,1,0:T(8,128)(2,1)}) %all-gather.6.cloned.1.call-update) | async-done | bytes 5242896 | tf_op jit(solution)/shard_map/all_gather | solution.py:101
  428.0 12.6 %reshape.179 = bf16[8,512,5,128]{3,2,1,0:T(8,128)(2,1)} reshape(bf16[1,4096,640]{2,1,0:T(8,128)(2,1)} %all-gather.6.cloned.1.call-done) | data formatting | bytes 10485760 | tf_op jit(solution)/shard_map/reshape;reshape;squeeze | solution.py:38
  440.6 7.1 %copy.36 = bf16[8,512,5,128]{3,1,2,0:T(8,128)(2,1)} copy(bf16[8,512,5,128]{3,2,1,0:T(8,128)(2,1)} %reshape.179) | data formatting | bytes 10485760
  447.8 60.8 %while.3 = (s32[]{:T(128)}, f32[5,256]{1,0:T(8,128)S(1)}, f32[5,256]{1,0:T(8,128)S(1)}, f32[5,256,128]{2,1,0:T(8,128)}, s32[8]{0:T(128)S(1)}, /*index=5*/s32[]{:...) while((s32[]{:T(128)}, f32[5,256]{1,0:T(8,128)S(1)}, ...), condition=%wide.region_7.8_spmd.clone, body=%wide.region_4.7_spmd.clone.sunk | while | flops 343252224 | bytes 16141529 | solution.py:65
  449.5 1.6 bitcast_reduce_fusion.2
  452.3 2.1 fusion.71
  454.5 0.9 copy-done.2
  457.1 1.6 bitcast_reduce_fusion.2
  459.9 2.1 fusion.71
  462.1 0.9 copy-done.2
  464.8 1.6 bitcast_reduce_fusion.2
  467.5 2.1 fusion.71
  469.7 0.9 copy-done.2
  472.4 1.6 bitcast_reduce_fusion.2
  475.1 2.1 fusion.71
  477.3 0.9 copy-done.2
  480.0 1.6 bitcast_reduce_fusion.2
  482.7 2.1 fusion.71
  484.9 0.9 copy-done.2
  487.6 1.6 bitcast_reduce_fusion.2
  490.3 2.1 fusion.71
  492.5 0.9 copy-done.2
  495.2 1.6 bitcast_reduce_fusion.2
  497.9 2.1 fusion.71
  500.1 0.9 copy-done.2
  502.8 1.6 bitcast_reduce_fusion.2
  505.5 2.1 fusion.71
  507.7 0.9 copy-done.2
  508.6 1.3 copy.39
  510.0 0.9 copy.45
  (117 shorter events, 23.5 us)
Async XLA Ops:
  7.2 118.0 %copy-start.3 = (f32[640]{0:T(1024)S(1)}, f32[640]{0:T(1024)}, u32[]{:S(2)}) copy-start(f32[640]{0:T(1024)} %param.23) | copy-start | bytes 7684
  7.2 87.9 %all-gather.10.cloned.1.call-start = ((), (), s32[]{:S(2)}) async-start(), calls=%async_computation.2 | async-start | bytes 1392640 | tf_op jit(solution)/shard_map/all_gather | solution.py:115
  7.9 224.7 %all-gather.8.cloned.1.call-start = ((), (), s32[]{:S(2)}) async-start(), calls=%async_computation.1 | async-start | bytes 5570560 | tf_op jit(solution)/shard_map/all_gather | solution.py:102
  8.7 288.4 %all-gather.12.cloned.1.call-start = ((), (), s32[]{:S(2)}) async-start(), calls=%async_computation.3 | async-start | bytes 6553600 | tf_op jit(solution)/shard_map/all_gather | solution.py:119
  125.2 2.8 copy-start
  125.2 2.8 copy-start.4
  126.6 2.3 copy-start.7
  126.6 4.9 copy-start.8
  126.6 5.5 %copy-start.9 = (s32[4]{0:T(128)S(1)}, s32[4]{0:T(128)}, u32[]{:S(2)}) copy-start(s32[4]{0:T(128)} %param.19) | copy-start | bytes 52
  126.6 6.7 %copy-start.5 = (f32[640]{0:T(1024)S(1)}, f32[640]{0:T(1024)}, u32[]{:S(2)}) copy-start(f32[640]{0:T(1024)} %param.17) | copy-start | bytes 7684
  127.9 300.1 %all-gather.6.cloned.1.call-start = ((), (), s32[]{:S(2)}) async-start(), calls=%async_computation | async-start | bytes 5570560 | tf_op jit(solution)/shard_map/all_gather | solution.py:101
  297.0 1.9 copy-start.6
  451.2 1.1 copy-start.1
  454.4 0.9 copy-start.2
  458.8 1.1 copy-start.1
  462.0 0.9 copy-start.2
  466.4 1.1 copy-start.1
  469.7 0.9 copy-start.2
  474.0 1.1 copy-start.1
  477.3 0.9 copy-start.2
  481.6 1.1 copy-start.1
  484.9 0.9 copy-start.2
  489.2 1.1 copy-start.1
  492.5 0.9 copy-start.2
  496.8 1.1 copy-start.1
  500.1 0.9 copy-start.2
  504.4 1.1 copy-start.1
  507.7 0.9 copy-start.2
Sparse Core Ops, SparseCore 0:
  10.1 84.9 all-gather.9
  97.1 135.4 all-gather.7
  234.7 62.2 all-gather.11
  299.5 128.4 all-gather.5
where the time goes:
time: 520 us; the launch traced here: 517 us
  waiting for transfers between devices  353 us (68%)
  local copies, waits for them, and re-layouts  64.9 us (12%)
  matrix products  32.1 us (6%)
  blocking collectives  27.6 us (5%)
  other arithmetic  17.7 us (3%)
  between operations  16 us (3%)
  loops' own time  5.74 us (1%)
    all_gather x1, waiting for transfers between devices, per_device(): keys = lax.all_gather(k_hat[None], 'seq', axis=1, tiled=True)  126 us
    all_gather x1, waiting for transfers between devices, per_device(): values = lax.all_gather(v_self, 'seq', axis=1, tiled=True)  98.9 us
    all_gather x1, waiting for transfers between devices, per_device(): whole = lax.all_gather(cap_kv, 'seq', axis=2, tiled=True)  82.7 us
    all_gather x1, waiting for transfers between devices, per_device(): routed = lax.all_gather(assembled, 'section', axis=1, tiled=True)  44.5 us
    psum x1, blocking collectives, per_device(): lax.psum((square_sums(q_self[0]), square_sums(k_self[0]), square_sums(q_c...  27.6 us
    unnamed x23, local copies, waits for them, and re-layouts  18.7 us
    dot_general x9, matrix products, one_block(): jnp.einsum('hqk,khd->hqd', weights.astype(jnp.bfloat16), value_block, pre...  18 us
    dot_general x9, matrix products, one_block(): jnp.einsum('qhd,khd->hqk', queries, key_block, preferred_element_type=jnp...  14.2 us
  transfers between devices with their start and end apart: 4, of which 4 were waited for; matrix products, arithmetic and copies ran while one was open for 7% of the time, Pallas kernels for 0%

commit v1 on v0

v1 whole, which is shorter than its diff:
```python
import functools
import math

import jax
import jax.numpy as jnp
from jax import lax
from jax.experimental import pallas as pl
from jax.experimental.pallas import tpu as pltpu
from jax.sharding import PartitionSpec as P

D = 5120
HEAD = 128
MESH = pl.DeviceIdType.MESH
MASKED = -1e30
PER_HEAD = 3
STEP = 80
PIECE = 96
EXTRA = PIECE - STEP


def square_sums(values):
    floats = values.astype(jnp.float32)
    return jnp.sum(floats * floats, axis=-1)


def scaled_rows(values, total_squares, gain):
    floats = values.astype(jnp.float32)
    factor = lax.rsqrt(total_squares / D + 1e-06)
    return (floats * factor[:, None] * gain[None, :]).astype(jnp.bfloat16)


def attend(q, key_ref, value_ref, bias_ref, slots):
    total_slots, rows, _ = key_ref.shape
    block = slots * rows
    scale = math.log2(math.e) / math.sqrt(HEAD)

    def body(number, carry):
        top, total, accum = carry
        keys = key_ref[pl.ds(number * slots, slots)].reshape(block, HEAD)
        values = value_ref[pl.ds(number * slots, slots)].reshape(block, HEAD)
        scores = lax.dot_general(
            q, keys, (((1,), (1,)), ((), ())), preferred_element_type=jnp.float32
        )
        start = pl.multiple_of(number * block, 128)
        scores = scores + bias_ref[0:1, pl.ds(start, block)]
        newest = jnp.maximum(top, jnp.max(scores, axis=-1, keepdims=True))
        weights = jnp.exp2((scores - newest) * scale)
        rescale = jnp.exp2((top - newest) * scale)
        total = total * rescale + jnp.sum(weights, axis=-1, keepdims=True)
        accum = accum * rescale + jnp.dot(
            weights.astype(jnp.bfloat16), values, preferred_element_type=jnp.float32
        )
        return (newest, total, accum)

    count = q.shape[0]
    state = (
        jnp.full((count, 1), MASKED, jnp.float32),
        jnp.zeros((count, 1), jnp.float32),
        jnp.zeros((count, HEAD), jnp.float32),
    )
    top, total, accum = lax.fori_loop(0, total_slots // slots, body, state)
    return (accum / total).astype(jnp.bfloat16)


def main_kernel(
    n, heads_here,
    limits, q, k, v, cq, ck, cv,
    out_self, out_cross,
    kr, vr, qr, ckr, cvr, cqr, os_buf, oc_buf, bias, cbias,
    send, recv, local, osend, orecv, olocal,
):
    me = lax.axis_index("seq")
    owners = heads_here * PER_HEAD
    barrier = pltpu.get_barrier_semaphore()

    @pl.loop(1, n)
    def _(d):
        pl.semaphore_signal(
            barrier, inc=1, device_id={"seq": lax.rem(me + d, n)}, device_id_type=MESH
        )

    pl.semaphore_wait(barrier, n - 1)

    def pieces(target):
        columns = pl.ds(pl.multiple_of((target // PER_HEAD) * HEAD, HEAD), HEAD)
        part = pl.ds(pl.multiple_of((target % PER_HEAD) * STEP, 16), PIECE)
        return (
            (k.at[:, columns], kr),
            (v.at[:, columns], vr),
            (q.at[part, columns], qr),
            (ck.at[:, columns], ckr),
            (cv.at[:, columns], cvr),
            (cq.at[part, columns], cqr),
        )

    def copies(d):
        target = lax.rem(me + d, n)
        return [
            pltpu.make_async_remote_copy(
                source, landing.at[me], send.at[d, number], recv.at[d, number],
                device_id={"seq": target}, device_id_type=MESH,
            )
            for number, (source, landing) in enumerate(pieces(target))
        ]

    def own_copies():
        return [
            pltpu.make_async_copy(source, landing.at[me], local.at[number])
            for number, (source, landing) in enumerate(pieces(me))
        ]

    @pl.loop(1, n)
    def _(d):
        @pl.when(lax.rem(me + d, n) < owners)
        def _():
            for copy in copies(d):
                copy.start()

    @pl.when(me < owners)
    def _():
        for copy in own_copies():
            copy.start()

    position = lax.broadcasted_iota(jnp.int32, bias.shape, 1)
    bias[...] = jnp.where(position < limits[0], 0.0, MASKED)
    position = lax.broadcasted_iota(jnp.int32, cbias.shape, 1)
    cbias[...] = jnp.where(position < limits[1], 0.0, MASKED)

    def arrivals(d):
        for number, landing in enumerate((kr, vr, qr, ckr, cvr, cqr)):
            pltpu.make_async_remote_copy(
                landing.at[0], landing.at[0], send.at[d, number], recv.at[d, number],
                device_id={"seq": lax.rem(me + 1, n)}, device_id_type=MESH,
            ).wait_recv()

    columns = pl.ds(pl.multiple_of((me // PER_HEAD) * HEAD, HEAD), HEAD)
    third = me % PER_HEAD

    def results(d, to, make):
        rows = pl.ds(pl.multiple_of(third * STEP + EXTRA, 16), STEP)
        found = []
        for number, (buf, out) in enumerate(((os_buf, out_self), (oc_buf, out_cross))):
            found.append(
                make(buf.at[to, pl.ds(EXTRA, STEP)], out.at[rows, columns], d, 2 * number)
            )
        return found

    def first_rows(d, to, make):
        found = []
        for number, (buf, out) in enumerate(((os_buf, out_self), (oc_buf, out_cross))):
            found.append(
                make(buf.at[to, pl.ds(0, EXTRA)], out.at[pl.ds(0, EXTRA), columns], d, 2 * number + 1)
            )
        return found

    def remote(source, landing, d, number):
        return pltpu.make_async_remote_copy(
            source, landing, osend.at[d, number], orecv.at[d, number],
            device_id={"seq": lax.rem(me + d, n)}, device_id_type=MESH,
        )

    def nearby(source, landing, d, number):
        return pltpu.make_async_copy(source, landing, olocal.at[number])

    @pl.when(me < owners)
    def _():
        for copy in own_copies():
            copy.wait()

        @pl.loop(1, n)
        def _(d):
            arrivals(d)

        group = 4
        @pl.loop(0, n // group)
        def _(g):
            queries = qr[pl.ds(g * group, group)].reshape(group * PIECE, HEAD)
            os_buf[pl.ds(g * group, group)] = attend(queries, kr, vr, bias, 4).reshape(
                group, PIECE, HEAD
            )
            queries = cqr[pl.ds(g * group, group)].reshape(group * PIECE, HEAD)
            oc_buf[pl.ds(g * group, group)] = attend(queries, ckr, cvr, cbias, 16).reshape(
                group, PIECE, HEAD
            )

        @pl.loop(1, n)
        def _(d):
            for copy in results(d, lax.rem(me + d, n), remote):
                copy.start()

            @pl.when(third == 0)
            def _():
                for copy in first_rows(d, lax.rem(me + d, n), remote):
                    copy.start()

        for copy in results(0, me, nearby):
            copy.start()

        @pl.when(third == 0)
        def _():
            for copy in first_rows(0, me, nearby):
                copy.start()

    @pl.loop(1, n)
    def _(d):
        @pl.when(lax.rem(me + d, n) < owners)
        def _():
            for copy in copies(d):
                copy.wait_send()

        sender = lax.rem(me + n - d, n)
        for number, out in ((0, out_self), (2, out_cross)):
            @pl.when(sender < owners)
            def _():
                piece = out.at[pl.ds(0, STEP), pl.ds(0, HEAD)]
                remote(piece, piece, d, number).wait_recv()

            @pl.when((sender < owners) & (sender % PER_HEAD == 0))
            def _():
                piece = out.at[pl.ds(0, EXTRA), pl.ds(0, HEAD)]
                remote(piece, piece, d, number + 1).wait_recv()

    @pl.when(me < owners)
    def _():
        for copy in results(0, me, nearby):
            copy.wait()

        @pl.when(third == 0)
        def _():
            for copy in first_rows(0, me, nearby):
                copy.wait()

        @pl.loop(1, n)
        def _(d):
            for copy in results(d, lax.rem(me + d, n), remote):
                copy.wait_send()

            @pl.when(third == 0)
            def _():
                for copy in first_rows(d, lax.rem(me + d, n), remote):
                    copy.wait_send()


def exchange_and_attend(limits, q, k, v, cq, ck, cv):
    n = lax.axis_size("seq")
    rows, width = q.shape
    cap_rows = ck.shape[0]
    bf16 = jnp.bfloat16
    vmem = pl.BlockSpec(memory_space=pltpu.VMEM)
    return pl.pallas_call(
        functools.partial(main_kernel, n, width // HEAD),
        out_shape=(
            jax.ShapeDtypeStruct((rows, width), bf16),
            jax.ShapeDtypeStruct((rows, width), bf16),
        ),
        in_specs=[pl.BlockSpec(memory_space=pltpu.SMEM)] + [vmem] * 6,
        out_specs=(vmem, vmem),
        scratch_shapes=[
            pltpu.VMEM((n, rows, HEAD), bf16),
            pltpu.VMEM((n, rows, HEAD), bf16),
            pltpu.VMEM((n, PIECE, HEAD), bf16),
            pltpu.VMEM((n, cap_rows, HEAD), bf16),
            pltpu.VMEM((n, cap_rows, HEAD), bf16),
            pltpu.VMEM((n, PIECE, HEAD), bf16),
            pltpu.VMEM((n, PIECE, HEAD), bf16),
            pltpu.VMEM((n, PIECE, HEAD), bf16),
            pltpu.VMEM((8, n * rows), jnp.float32),
            pltpu.VMEM((8, n * cap_rows), jnp.float32),
            pltpu.SemaphoreType.DMA((n, 6)),
            pltpu.SemaphoreType.DMA((n, 6)),
            pltpu.SemaphoreType.DMA((6,)),
            pltpu.SemaphoreType.DMA((n, 4)),
            pltpu.SemaphoreType.DMA((n, 4)),
            pltpu.SemaphoreType.DMA((4,)),
        ],
        compiler_params=pltpu.CompilerParams(
            collective_id=0, has_side_effects=True, vmem_limit_bytes=56 << 20
        ),
    )(limits, q, k, v, cq, ck, cv)


def per_device(
    q_self,
    k_self,
    v_self,
    gain_q_self,
    gain_k_self,
    counts,
    q_cross,
    cap_kv,
    gain_q_cross,
    gain_k_cross,
    cap_len,
    owner,
):
    section = lax.axis_index("section")
    numbers = jnp.arange(lax.axis_size("section"), dtype=jnp.int32)
    source = jnp.sum(jnp.where(owner == section, numbers, 0))
    limits = jnp.stack([counts[section], cap_len[source]])
    captions = lax.all_gather(cap_kv, "section", axis=1, tiled=True)
    caption = lax.dynamic_index_in_dim(captions, source, 1, keepdims=False)
    totals = lax.psum(
        (
            square_sums(q_self[0]),
            square_sums(k_self[0]),
            square_sums(q_cross[0]),
            square_sums(caption[0]),
        ),
        "wide",
    )
    out_self, out_cross = exchange_and_attend(
        limits,
        scaled_rows(q_self[0], totals[0], gain_q_self),
        scaled_rows(k_self[0], totals[1], gain_k_self),
        v_self[0],
        scaled_rows(q_cross[0], totals[2], gain_q_cross),
        scaled_rows(caption[0], totals[3], gain_k_cross),
        caption[1],
    )
    return (out_self[None], out_cross[None])


def solution(mesh):
    whole = P("section", "seq", "wide")
    return jax.shard_map(
        per_device,
        mesh=mesh,
        in_specs=(
            whole, whole, whole, P("wide"), P("wide"), P(), whole,
            P(None, "section", "seq", "wide"), P("wide"), P("wide"), P(), P(),
        ),
        out_specs=(whole, whole),
        check_vma=False,
    )
```

time: 520 us -> 163 us (0.31)
  the two profiles are of different devices: /device:TPU:1 before, /device:TPU:106 now
where the time goes in v1:
time: 163 us; the launch traced here: 162 us
  Pallas kernels  109 us (67%)
  blocking collectives  34.9 us (21%)
  other arithmetic  8.12 us (5%)
  local copies, waits for them, and re-layouts  7.2 us (4%)
  between operations  2.66 us (2%)
    pallas_call x1, Pallas kernels, exchange_and_attend(): pl.pallas_call(functools.partial(main_kernel, n, width // HEAD), out_shap...  109 us
    psum x1, blocking collectives, per_device(): lax.psum((square_sums(q_self[0]), square_sums(k_self[0]), square_sums(q_c...  22.3 us
    all_gather x1, blocking collectives, per_device(): captions = lax.all_gather(cap_kv, 'section', axis=1, tiled=True)  12.6 us
    unnamed x20, local copies, waits for them, and re-layouts  4.12 us
    convert_element_type x4, other arithmetic, scaled_rows(): return (floats * factor[:, None] * gain[None, :]).astype(jnp.bfloat16)  3.29 us

profile of v1, /device:TPU:106, one launch (start us, length us, event | category | flops | bytes accessed | tf_op | source)
XLA Modules:
  0.0 162.4 jit_solution(11602412898431129676)
XLA Ops:
  0.6 0.0 copy-start.2
  0.6 1.3 fusion.12
  3.9 1.2 dynamic_slice.11
  5.2 1.2 dynamic_slice.10
  6.4 1.9 %pad_add_fusion.limits = s32[2]{0:T(128)} fusion(s32[1]{0:T(128)} %dynamic_slice.11, s32[1]{0:T(128)} %dynamic_slice.10), kind=kLoop, calls=%fused_computation.27 | loop fusion | flops 2 | bytes 16 | tf_op jit(solution)/shard_map/stack | solution.py:299
  8.3 0.0 copy-start
  8.3 1.2 fusion
  9.5 0.0 copy-done.2
  9.5 0.1 fusion.3
  9.6 0.0 copy-done
  9.6 0.0 copy-start.4
  9.6 0.1 fusion.6
  9.8 0.7 copy-done.4
  10.5 12.6 %all_gather.3 = bf16[2,4,32,640]{3,2,1,0:T(8,128)(2,1)S(1)} all-gather(bf16[2,1,32,640]{3,2,1,0:T(8,128)(2,1)S(1)} %copy-done.4), channel_id=1, replica_groups=mesh['section'=4,'seq'=16,'wide'=8] {'section'}, dimensions={1}, use_global_device_ids=true | all-gather | bytes 409600 | tf_op jit(solution)/shard_map/all_gather | solution.py:300
  23.2 0.1 fusion.9
  23.3 22.3 %all-reduce = (f32[256]{0:T(256)S(1)}, f32[256]{0:T(256)S(1)}, f32[256]{0:T(256)S(1)}, f32[32]{0:T(128)S(1)}) all-reduce(f32[256]{0:T(256)S(1)} %fusion, f32[256]{0:T(256)S(1)} %fusion.3, f32[256]{0:T(256)S(1)} %fusion.6, f32[32]{0:T(128)S(1)} %fusion.9), channel_id=1, replica_groups=mesh['section'=4,'seq'=16,'wide'=8] {'wide'}, use_global_device_ids=true, to_apply=%region_2.3 | all-reduce | flops 800 | bytes 6400 | tf_op jit(solution)/shard_map/psum | solution.py:302
  45.6 0.0 copy-start.8
  45.6 0.7 copy-done.8
  46.3 0.7 fusion.11.ck
  47.0 0.0 copy-start.5
  47.0 0.6 dynamic-slice_bitcast_fusion.cv
  47.6 0.1 copy-done.5
  47.6 0.0 copy-start.1
  47.7 0.0 copy-start.6
  47.7 0.9 fusion.8.cq
  48.5 0.1 copy-done.1
  48.6 0.0 copy-done.6
  48.6 0.0 copy-start.7
  48.6 0.9 fusion.2.q
  49.5 0.0 copy-done.7
  49.5 0.9 fusion.5.k
  50.4 109.5 %shard_map.131 = (bf16[256,640]{1,0:T(8,128)(2,1)}, bf16[256,640]{1,0:T(8,128)(2,1)}) custom-call(s32[2]{0:T(128)} %pad_add_fusion.limits, bf16[256,640]{1,0:T(8,128)(2,1)} %fusion.2.q, bf16[256,640]{1,0:T(8,128)(2,1)} %fusion.5.k, bf16[256,640]{1,0:T(8,128)(2,1)} %bitcast.24, bf16[256,640]{1,0:T(8,128)(2,1)} %fusion.8.cq, bf16[32,640]{1,0:T(8,128)(2,1)} %fusion.11.ck, ...), custom_call_target="tpu_custom_call" | custom-call | tf_op jit(solution)/shard_map/pallas_call | solution.py:250
  159.9 0.0 copy-start.3
  159.9 1.8 %copy.16 = bf16[1,256,640]{2,1,0:T(8,128)(2,1)} copy(bf16[1,256,640]{2,1,0:T(8,128)(2,1)} %bitcast.26) | data formatting | bytes 655360
  161.6 0.0 copy-done.3
  161.6 0.7 copy.17
  (3 shorter events, 0.0 us)
Async XLA Ops:
  0.6 8.8 %copy-start.2 = (bf16[1,256,640]{2,1,0:T(8,128)(2,1)S(1)}, bf16[1,256,640]{2,1,0:T(8,128)(2,1)}, u32[]{:S(2)}) copy-start(bf16[1,256,640]{2,1,0:T(8,128)(2,1)} %param.13) | copy-start | bytes 983044
  8.3 1.3 copy-start
  9.6 0.9 copy-start.4
  45.6 0.7 copy-start.8
  47.0 0.7 copy-start.5
  47.6 1.0 copy-start.1
  47.7 1.0 copy-start.6
  48.6 0.9 copy-start.7
  159.9 1.8 %copy-start.3 = (bf16[256,640]{1,0:T(8,128)(2,1)S(1)}, bf16[256,640]{1,0:T(8,128)(2,1)}, u32[]{:S(2)}) copy-start(bf16[256,640]{1,0:T(8,128)(2,1)} %get-tuple-element.5) | copy-start | bytes 983044

commit v2 on v1

--- a/solution.py
+++ b/solution.py
@@ -18,15 +18,13 @@
 EXTRA = PIECE - STEP
 
 
-def square_sums(values):
-    floats = values.astype(jnp.float32)
-    return jnp.sum(floats * floats, axis=-1)
-
-
-def scaled_rows(values, total_squares, gain):
-    floats = values.astype(jnp.float32)
-    factor = lax.rsqrt(total_squares / D + 1e-06)
-    return (floats * factor[:, None] * gain[None, :]).astype(jnp.bfloat16)
+def square_sums(ref):
+    floats = ref.astype(jnp.float32)
+    return jnp.sum(floats * floats, axis=-1, keepdims=True)
+
+
+def scaled_rows(values, factor, gain):
+    return (values.astype(jnp.float32) * factor * gain).astype(jnp.bfloat16)
 
 
 def attend(q, key_ref, value_ref, bias_ref, slots):
@@ -63,23 +61,27 @@
 
 
 def main_kernel(
-    n, heads_here,
-    limits, q, k, v, cq, ck, cv,
+    n, sections, wides, heads_here,
+    counts, cap_len, owner, q_raw, k_raw, v, cq_raw, cap, gq, gk, gcq, gck,
     out_self, out_cross,
     kr, vr, qr, ckr, cvr, cqr, os_buf, oc_buf, bias, cbias,
-    send, recv, local, osend, orecv, olocal,
+    q, k, cq, capr, chosen, columns_of, stat, stats, factors,
+    send, recv, local, osend, orecv, olocal, wsend, wrecv, ssend, srecv,
 ):
     me = lax.axis_index("seq")
+    section = lax.axis_index("section")
+    wide = lax.axis_index("wide")
     owners = heads_here * PER_HEAD
     barrier = pltpu.get_barrier_semaphore()
-
-    @pl.loop(1, n)
-    def _(d):
-        pl.semaphore_signal(
-            barrier, inc=1, device_id={"seq": lax.rem(me + d, n)}, device_id_type=MESH
-        )
-
-    pl.semaphore_wait(barrier, n - 1)
+    for axis, here, size in (("seq", me, n), ("section", section, sections), ("wide", wide, wides)):
+        @pl.loop(1, size)
+        def _(d):
+            pl.semaphore_signal(
+                barrier, inc=1, device_id={axis: lax.rem(here + d, size)}, device_id_type=MESH
+            )
+
+    pl.semaphore_wait(barrier, n + sections + wides - 3)
+    ck, cv = chosen.at[0], chosen.at[1]
 
     def pieces(target):
         columns = pl.ds(pl.multiple_of((target // PER_HEAD) * HEAD, HEAD), HEAD)
@@ -93,38 +95,102 @@
             (cq.at[part, columns], cqr),
         )
 
-    def copies(d):
+    def copies(d, numbers=range(6)):
         target = lax.rem(me + d, n)
         return [
             pltpu.make_async_remote_copy(
                 source, landing.at[me], send.at[d, number], recv.at[d, number],
                 device_id={"seq": target}, device_id_type=MESH,
             )
-            for number, (source, landing) in enumerate(pieces(target))
+            for number, (source, landing) in enumerate(pieces(target)) if number in numbers
         ]
 
-    def own_copies():
+    def own_copies(numbers=range(6)):
         return [
             pltpu.make_async_copy(source, landing.at[me], local.at[number])
-            for number, (source, landing) in enumerate(pieces(me))
+            for number, (source, landing) in enumerate(pieces(me)) if number in numbers
         ]
 
-    @pl.loop(1, n)
+    def start(numbers):
+        @pl.loop(1, n)
+        def _(d):
+            @pl.when(lax.rem(me + d, n) < owners)
+            def _():
+                for copy in copies(d, numbers):
+                    copy.start()
+
+        @pl.when(me < owners)
+        def _():
+            for copy in own_copies(numbers):
+                copy.start()
+
+    def to_section(d, number):
+        return pltpu.make_async_remote_copy(
+            (cap if number == 1 else capr.at[section]).at[number],
+            capr.at[section, number], ssend.at[d, number], srecv.at[d, number],
+            device_id={"section": lax.rem(section + d, sections)}, device_id_type=MESH,
+        )
+
+    def to_wide(d):
+        return pltpu.make_async_remote_copy(
+            stat, stats.at[wide], wsend.at[d], wrecv.at[d],
+            device_id={"wide": lax.rem(wide + d, wides)}, device_id_type=MESH,
+        )
+
+    cap_rows = cap.shape[1]
+    lane = lax.broadcasted_iota(jnp.int32, columns_of.shape, 1)
+    columns_of[...] = jnp.where(
+        lane == 0, square_sums(q_raw[...]),
+        jnp.where(lane == 1, square_sums(k_raw[...]),
+                  jnp.where(lane == 2, square_sums(cq_raw[...]), 0.0)),
+    )
+    columns_of[0:cap_rows] = jnp.where(
+        lane[0:cap_rows] == 3, square_sums(cap[0]), columns_of[0:cap_rows]
+    )
+    partial = columns_of[...].T[0:8]
+    stat[...] = partial
+    stats[wide] = partial
+    capr[section, 1] = cap[1]
+    factors[...] = jnp.zeros(factors.shape, jnp.float32)
+
+    @pl.loop(1, wides)
     def _(d):
-        @pl.when(lax.rem(me + d, n) < owners)
-        def _():
-            for copy in copies(d):
-                copy.start()
-
-    @pl.when(me < owners)
-    def _():
-        for copy in own_copies():
-            copy.start()
-
+        to_wide(d).start()
+
+    start((1,))
+    for d in range(1, sections):
+        to_section(d, 1).start()
+
+    source = section * 0
+    for s in range(sections):
+        source = jnp.where(owner[s] == section, s, source)
     position = lax.broadcasted_iota(jnp.int32, bias.shape, 1)
-    bias[...] = jnp.where(position < limits[0], 0.0, MASKED)
+    bias[...] = jnp.where(position < counts[section], 0.0, MASKED)
     position = lax.broadcasted_iota(jnp.int32, cbias.shape, 1)
-    cbias[...] = jnp.where(position < limits[1], 0.0, MASKED)
+    cbias[...] = jnp.where(position < cap_len[source], 0.0, MASKED)
+
+    @pl.loop(1, wides)
+    def _(d):
+        to_wide(d).wait_recv()
+
+    total = stats[0]
+    for w in range(1, wides):
+        total = total + stats[w]
+    factors[0:8] = lax.rsqrt(total / D + 1e-06)
+    factor = factors[...].T
+    capr[section, 0] = scaled_rows(cap[0], factor[0:cap_rows, 3:4], gck[...])
+    k[...] = scaled_rows(k_raw[...], factor[:, 1:2], gk[...])
+    q[...] = scaled_rows(q_raw[...], factor[:, 0:1], gq[...])
+    cq[...] = scaled_rows(cq_raw[...], factor[:, 2:3], gcq[...])
+    for d in range(1, sections):
+        to_section(d, 0).start()
+    start((0,))
+    start((2, 5))
+    for d in range(1, sections):
+        for number in range(2):
+            to_section(d, number).wait_recv()
+    chosen[...] = capr[source]
+    start((3, 4))
 
     def arrivals(d):
         for number, landing in enumerate((kr, vr, qr, ckr, cvr, cqr)):
@@ -220,6 +286,14 @@
                 piece = out.at[pl.ds(0, EXTRA), pl.ds(0, HEAD)]
                 remote(piece, piece, d, number + 1).wait_recv()
 
+    @pl.loop(1, wides)
+    def _(d):
+        to_wide(d).wait_send()
+
+    for d in range(1, sections):
+        for number in range(2):
+            to_section(d, number).wait_send()
+
     @pl.when(me < owners)
     def _():
         for copy in results(0, me, nearby):
@@ -241,19 +315,20 @@
                     copy.wait_send()
 
 
-def exchange_and_attend(limits, q, k, v, cq, ck, cv):
-    n = lax.axis_size("seq")
+def exchange_and_attend(counts, cap_len, owner, q, k, v, cq, cap, gq, gk, gcq, gck):
+    n, sections, wides = (lax.axis_size(axis) for axis in ("seq", "section", "wide"))
     rows, width = q.shape
-    cap_rows = ck.shape[0]
-    bf16 = jnp.bfloat16
+    cap_rows = cap.shape[1]
+    bf16, f32 = jnp.bfloat16, jnp.float32
     vmem = pl.BlockSpec(memory_space=pltpu.VMEM)
+    dma = pltpu.SemaphoreType.DMA
     return pl.pallas_call(
-        functools.partial(main_kernel, n, width // HEAD),
+        functools.partial(main_kernel, n, sections, wides, width // HEAD),
         out_shape=(
             jax.ShapeDtypeStruct((rows, width), bf16),
             jax.ShapeDtypeStruct((rows, width), bf16),
         ),
-        in_specs=[pl.BlockSpec(memory_space=pltpu.SMEM)] + [vmem] * 6,
+        in_specs=[pl.BlockSpec(memory_space=pltpu.SMEM)] * 3 + [vmem] * 9,
         out_specs=(vmem, vmem),
         scratch_shapes=[
             pltpu.VMEM((n, rows, HEAD), bf16),
@@ -264,19 +339,26 @@
             pltpu.VMEM((n, PIECE, HEAD), bf16),
             pltpu.VMEM((n, PIECE, HEAD), bf16),
             pltpu.VMEM((n, PIECE, HEAD), bf16),
-            pltpu.VMEM((8, n * rows), jnp.float32),
-            pltpu.VMEM((8, n * cap_rows), jnp.float32),
-            pltpu.SemaphoreType.DMA((n, 6)),
-            pltpu.SemaphoreType.DMA((n, 6)),
-            pltpu.SemaphoreType.DMA((6,)),
-            pltpu.SemaphoreType.DMA((n, 4)),
-            pltpu.SemaphoreType.DMA((n, 4)),
-            pltpu.SemaphoreType.DMA((4,)),
+            pltpu.VMEM((8, n * rows), f32),
+            pltpu.VMEM((8, n * cap_rows), f32),
+            pltpu.VMEM((rows, width), bf16),
+            pltpu.VMEM((rows, width), bf16),
+            pltpu.VMEM((rows, width), bf16),
+            pltpu.VMEM((sections, 2, cap_rows, width), bf16),
+            pltpu.VMEM((2, cap_rows, width), bf16),
+            pltpu.VMEM((rows, HEAD), f32),
+            pltpu.VMEM((8, rows), f32),
+            pltpu.VMEM((wides, 8, rows), f32),
+            pltpu.VMEM((HEAD, rows), f32),
+            dma((n, 6)), dma((n, 6)), dma((6,)),
+            dma((n, 4)), dma((n, 4)), dma((4,)),
+            dma((wides,)), dma((wides,)),
+            dma((sections, 2)), dma((sections, 2)),
         ],
         compiler_params=pltpu.CompilerParams(
             collective_id=0, has_side_effects=True, vmem_limit_bytes=56 << 20
         ),
-    )(limits, q, k, v, cq, ck, cv)
+    )(counts, cap_len, owner, q, k, v, cq, cap, gq, gk, gcq, gck)
 
 
 def per_device(
@@ -293,29 +375,10 @@
     cap_len,
     owner,
 ):
-    section = lax.axis_index("section")
-    numbers = jnp.arange(lax.axis_size("section"), dtype=jnp.int32)
-    source = jnp.sum(jnp.where(owner == section, numbers, 0))
-    limits = jnp.stack([counts[section], cap_len[source]])
-    captions = lax.all_gather(cap_kv, "section", axis=1, tiled=True)
-    caption = lax.dynamic_index_in_dim(captions, source, 1, keepdims=False)
-    totals = lax.psum(
-        (
-            square_sums(q_self[0]),
-            square_sums(k_self[0]),
-            square_sums(q_cross[0]),
-            square_sums(caption[0]),
-        ),
-        "wide",
-    )
     out_self, out_cross = exchange_and_attend(
-        limits,
-        scaled_rows(q_self[0], totals[0], gain_q_self),
-        scaled_rows(k_self[0], totals[1], gain_k_self),
-        v_self[0],
-        scaled_rows(q_cross[0], totals[2], gain_q_cross),
-        scaled_rows(caption[0], totals[3], gain_k_cross),
-        caption[1],
+        counts, cap_len, owner,
+        q_self[0], k_self[0], v_self[0], q_cross[0], cap_kv[:, 0],
+        gain_q_self[None], gain_k_self[None], gain_q_cross[None], gain_k_cross[None],
     )
     return (out_self[None], out_cross[None])
 

time: 163 us -> 134 us (0.82)
  the two profiles are of different devices: /device:TPU:106 before, /device:TPU:96 now
where the time goes in v2:
time: 134 us; the launch traced here: 133 us
  Pallas kernels  127 us (95%)
  local copies, waits for them, and re-layouts  5.72 us (4%)
    pallas_call x1, Pallas kernels, exchange_and_attend(): pl.pallas_call(functools.partial(main_kernel, n, sections, wides, width /...  127 us
    unnamed x12, local copies, waits for them, and re-layouts  3.4 us

profile of v2, /device:TPU:96, one launch (start us, length us, event | category | flops | bytes accessed | tf_op | source)
XLA Modules:
  0.0 133.3 jit_solution(3746267479032770915)
XLA Ops:
  0.6 0.0 copy-start.1
  0.6 0.0 copy-start.2
  0.6 0.7 copy-done.1
  1.3 0.6 broadcast_in_dim.18.gq
  1.9 0.0 copy-done.2
  1.9 0.0 copy-start.3
  1.9 0.6 broadcast_in_dim.19.gk
  2.5 0.1 copy-done.3
  2.6 0.0 copy-start.4
  2.6 0.6 broadcast_in_dim.20.gcq
  3.2 0.1 copy-done.4
  3.3 0.6 broadcast_in_dim.21.gck
  3.9 126.9 %shard_map.131 = (bf16[256,640]{1,0:T(8,128)(2,1)}, bf16[256,640]{1,0:T(8,128)(2,1)}) custom-call(s32[4]{0:T(128)} %counts.1, s32[4]{0:T(128)} %cap_len.1, s32[4]{0:T(128)} %owner.1, bf16[256,640]{1,0:T(8,128)(2,1)} %bitcast.9, bf16[256,640]{1,0:T(8,128)(2,1)} %bitcast.10, bf16[256,640]{1,0:T(8,128)(2,1)} %bitcast.11, bf16[256,640]{1,0:T(8,128)(2,1)} %bitcast.12, ...), custom_call_target="tpu_custom_call" | custom-call | tf_op jit(solution)/shard_map/pallas_call | solution.py:325
  130.8 0.0 copy-start
  130.8 1.8 %copy.16 = bf16[1,256,640]{2,1,0:T(8,128)(2,1)} copy(bf16[1,256,640]{2,1,0:T(8,128)(2,1)} %bitcast.8) | data formatting | bytes 655360
  132.5 0.0 copy-done
  132.5 0.7 copy.17
Async XLA Ops:
  0.6 0.7 copy-start.1
  0.6 1.3 copy-start.2
  1.9 0.7 copy-start.3
  2.6 0.7 copy-start.4
  130.8 1.8 %copy-start = (bf16[256,640]{1,0:T(8,128)(2,1)S(1)}, bf16[256,640]{1,0:T(8,128)(2,1)}, u32[]{:S(2)}) copy-start(bf16[256,640]{1,0:T(8,128)(2,1)} %get-tuple-element.5) | copy-start | bytes 983044

commit v3 on v2

--- a/solution.py
+++ b/solution.py
@@ -72,6 +72,13 @@
     section = lax.axis_index("section")
     wide = lax.axis_index("wide")
     owners = heads_here * PER_HEAD
+    side = math.isqrt(n)
+
+    def rank(index):
+        return (index % side) * side + index // side if side * side == n else index
+
+    mine = rank(me)
+    third = mine % PER_HEAD
     barrier = pltpu.get_barrier_semaphore()
     for axis, here, size in (("seq", me, n), ("section", section, sections), ("wide", wide, wides)):
         @pl.loop(1, size)
@@ -84,8 +91,8 @@
     ck, cv = chosen.at[0], chosen.at[1]
 
     def pieces(target):
-        columns = pl.ds(pl.multiple_of((target // PER_HEAD) * HEAD, HEAD), HEAD)
-        part = pl.ds(pl.multiple_of((target % PER_HEAD) * STEP, 16), PIECE)
+        columns = pl.ds(pl.multiple_of((rank(target) // PER_HEAD) * HEAD, HEAD), HEAD)
+        part = pl.ds(pl.multiple_of((rank(target) % PER_HEAD) * STEP, 16), PIECE)
         return (
             (k.at[:, columns], kr),
             (v.at[:, columns], vr),
@@ -114,12 +121,12 @@
     def start(numbers):
         @pl.loop(1, n)
         def _(d):
-            @pl.when(lax.rem(me + d, n) < owners)
+            @pl.when(rank(lax.rem(me + d, n)) < owners)
             def _():
                 for copy in copies(d, numbers):
                     copy.start()
 
-        @pl.when(me < owners)
+        @pl.when(mine < owners)
         def _():
             for copy in own_copies(numbers):
                 copy.start()
@@ -199,8 +206,7 @@
                 device_id={"seq": lax.rem(me + 1, n)}, device_id_type=MESH,
             ).wait_recv()
 
-    columns = pl.ds(pl.multiple_of((me // PER_HEAD) * HEAD, HEAD), HEAD)
-    third = me % PER_HEAD
+    columns = pl.ds(pl.multiple_of((mine // PER_HEAD) * HEAD, HEAD), HEAD)
 
     def results(d, to, make):
         rows = pl.ds(pl.multiple_of(third * STEP + EXTRA, 16), STEP)
@@ -228,7 +234,7 @@
     def nearby(source, landing, d, number):
         return pltpu.make_async_copy(source, landing, olocal.at[number])
 
-    @pl.when(me < owners)
+    @pl.when(mine < owners)
     def _():
         for copy in own_copies():
             copy.wait()
@@ -238,6 +244,23 @@
             arrivals(d)
 
         group = 4
+
+        def give(g):
+            @pl.loop(0, group)
+            def _(i):
+                to = g * group + i
+                d = lax.rem(to + n - me, n)
+                for near, make in ((True, nearby), (False, remote)):
+                    @pl.when((d == 0) if near else (d > 0))
+                    def _():
+                        for copy in results(d, to, make):
+                            copy.start()
+
+                        @pl.when(third == 0)
+                        def _():
+                            for copy in first_rows(d, to, make):
+                                copy.start()
+
         @pl.loop(0, n // group)
         def _(g):
             queries = qr[pl.ds(g * group, group)].reshape(group * PIECE, HEAD)
@@ -249,39 +272,28 @@
                 group, PIECE, HEAD
             )
 
-        @pl.loop(1, n)
-        def _(d):
-            for copy in results(d, lax.rem(me + d, n), remote):
-                copy.start()
-
-            @pl.when(third == 0)
+            @pl.when(g > 0)
             def _():
-                for copy in first_rows(d, lax.rem(me + d, n), remote):
-                    copy.start()
-
-        for copy in results(0, me, nearby):
-            copy.start()
-
-        @pl.when(third == 0)
-        def _():
-            for copy in first_rows(0, me, nearby):
-                copy.start()
+                give(g - 1)
+
+
+        give(n // group - 1)
 
     @pl.loop(1, n)
     def _(d):
-        @pl.when(lax.rem(me + d, n) < owners)
+        @pl.when(rank(lax.rem(me + d, n)) < owners)
         def _():
             for copy in copies(d):
                 copy.wait_send()
 
         sender = lax.rem(me + n - d, n)
         for number, out in ((0, out_self), (2, out_cross)):
-            @pl.when(sender < owners)
+            @pl.when(rank(sender) < owners)
             def _():
                 piece = out.at[pl.ds(0, STEP), pl.ds(0, HEAD)]
                 remote(piece, piece, d, number).wait_recv()
 
-            @pl.when((sender < owners) & (sender % PER_HEAD == 0))
+            @pl.when((rank(sender) < owners) & (rank(sender) % PER_HEAD == 0))
             def _():
                 piece = out.at[pl.ds(0, EXTRA), pl.ds(0, HEAD)]
                 remote(piece, piece, d, number + 1).wait_recv()
@@ -294,7 +306,7 @@
         for number in range(2):
             to_section(d, number).wait_send()
 
-    @pl.when(me < owners)
+    @pl.when(mine < owners)
     def _():
         for copy in results(0, me, nearby):
             copy.wait()

time: 134 us -> 125 us (0.933)
  the two profiles are of different devices: /device:TPU:96 before, /device:TPU:1 now
where the time goes in v3:
time: 125 us; the launch traced here: 124 us
  Pallas kernels  118 us (94%)
  local copies, waits for them, and re-layouts  5.72 us (5%)
    pallas_call x1, Pallas kernels, exchange_and_attend(): pl.pallas_call(functools.partial(main_kernel, n, sections, wides, width /...  118 us
    unnamed x12, local copies, waits for them, and re-layouts  3.4 us

profile of v3, /device:TPU:1, one launch (start us, length us, event | category | flops | bytes accessed | tf_op | source)
XLA Modules:
  0.0 124.1 jit_solution(3327565375465620834)
XLA Ops:
  0.6 0.0 copy-start.1
  0.6 0.0 copy-start.2
  0.6 0.7 copy-done.1
  1.3 0.6 broadcast_in_dim.18.gq
  1.9 0.0 copy-done.2
  1.9 0.0 copy-start.3
  1.9 0.6 broadcast_in_dim.19.gk
  2.5 0.1 copy-done.3
  2.6 0.0 copy-start.4
  2.6 0.6 broadcast_in_dim.20.gcq
  3.2 0.1 copy-done.4
  3.3 0.6 broadcast_in_dim.21.gck
  3.9 117.7 %shard_map.131 = (bf16[256,640]{1,0:T(8,128)(2,1)}, bf16[256,640]{1,0:T(8,128)(2,1)}) custom-call(s32[4]{0:T(128)} %counts.1, s32[4]{0:T(128)} %cap_len.1, s32[4]{0:T(128)} %owner.1, bf16[256,640]{1,0:T(8,128)(2,1)} %bitcast.9, bf16[256,640]{1,0:T(8,128)(2,1)} %bitcast.10, bf16[256,640]{1,0:T(8,128)(2,1)} %bitcast.11, bf16[256,640]{1,0:T(8,128)(2,1)} %bitcast.12, ...), custom_call_target="tpu_custom_call" | custom-call | tf_op jit(solution)/shard_map/pallas_call | solution.py:337
  121.6 0.0 copy-start
  121.6 1.8 %copy.16 = bf16[1,256,640]{2,1,0:T(8,128)(2,1)} copy(bf16[1,256,640]{2,1,0:T(8,128)(2,1)} %bitcast.8) | data formatting | bytes 655360
  123.4 0.0 copy-done
  123.4 0.7 copy.17
Async XLA Ops:
  0.6 0.7 copy-start.1
  0.6 1.3 %copy-start.2 = (f32[640]{0:T(1024)S(1)}, f32[640]{0:T(1024)}, u32[]{:S(2)}) copy-start(f32[640]{0:T(1024)} %param.16) | copy-start | bytes 7684
  1.9 0.7 copy-start.3
  2.6 0.7 copy-start.4
  121.6 1.8 %copy-start = (bf16[256,640]{1,0:T(8,128)(2,1)S(1)}, bf16[256,640]{1,0:T(8,128)(2,1)}, u32[]{:S(2)}) copy-start(bf16[256,640]{1,0:T(8,128)(2,1)} %get-tuple-element.5) | copy-start | bytes 983044

commit v4 on v3

--- a/solution.py
+++ b/solution.py
@@ -16,6 +16,7 @@
 STEP = 80
 PIECE = 96
 EXTRA = PIECE - STEP
+GROUPS = 4
 
 
 def square_sums(ref):
@@ -27,37 +28,35 @@
     return (values.astype(jnp.float32) * factor * gain).astype(jnp.bfloat16)
 
 
-def attend(q, key_ref, value_ref, bias_ref, slots):
-    total_slots, rows, _ = key_ref.shape
-    block = slots * rows
+def first_state(state):
+    top, total, accum = state
+    top[...] = jnp.full(top.shape, MASKED, jnp.float32)
+    total[...] = jnp.zeros(total.shape, jnp.float32)
+    accum[...] = jnp.zeros(accum.shape, jnp.float32)
+
+
+def attend(q_ref, keys, values, bias, state, after=None):
     scale = math.log2(math.e) / math.sqrt(HEAD)
-
-    def body(number, carry):
-        top, total, accum = carry
-        keys = key_ref[pl.ds(number * slots, slots)].reshape(block, HEAD)
-        values = value_ref[pl.ds(number * slots, slots)].reshape(block, HEAD)
+    groups, count, _ = q_ref.shape
+    top_ref, total_ref, accum_ref = state
+
+    @pl.loop(0, groups)
+    def _(g):
         scores = lax.dot_general(
-            q, keys, (((1,), (1,)), ((), ())), preferred_element_type=jnp.float32
-        )
-        start = pl.multiple_of(number * block, 128)
-        scores = scores + bias_ref[0:1, pl.ds(start, block)]
+            q_ref[g], keys, (((1,), (1,)), ((), ())), preferred_element_type=jnp.float32
+        ) + bias
+        top = top_ref[g][:, 0:1]
         newest = jnp.maximum(top, jnp.max(scores, axis=-1, keepdims=True))
         weights = jnp.exp2((scores - newest) * scale)
         rescale = jnp.exp2((top - newest) * scale)
-        total = total * rescale + jnp.sum(weights, axis=-1, keepdims=True)
-        accum = accum * rescale + jnp.dot(
+        total = total_ref[g][:, 0:1] * rescale + jnp.sum(weights, axis=-1, keepdims=True)
+        accum_ref[g] = accum_ref[g] * rescale + jnp.dot(
             weights.astype(jnp.bfloat16), values, preferred_element_type=jnp.float32
         )
-        return (newest, total, accum)
-
-    count = q.shape[0]
-    state = (
-        jnp.full((count, 1), MASKED, jnp.float32),
-        jnp.zeros((count, 1), jnp.float32),
-        jnp.zeros((count, HEAD), jnp.float32),
-    )
-    top, total, accum = lax.fori_loop(0, total_slots // slots, body, state)
-    return (accum / total).astype(jnp.bfloat16)
+        top_ref[g] = jnp.broadcast_to(newest, (count, HEAD))
+        total_ref[g] = jnp.broadcast_to(total, (count, HEAD))
+        if after is not None:
+            after(g)
 
 
 def main_kernel(
@@ -66,6 +65,7 @@
     out_self, out_cross,
     kr, vr, qr, ckr, cvr, cqr, os_buf, oc_buf, bias, cbias,
     q, k, cq, capr, chosen, columns_of, stat, stats, factors,
+    queries, top_w, total_w, accum,
     send, recv, local, osend, orecv, olocal, wsend, wrecv, ssend, srecv,
 ):
     me = lax.axis_index("seq")
@@ -106,7 +106,7 @@
         target = lax.rem(me + d, n)
         return [
             pltpu.make_async_remote_copy(
-                source, landing.at[me], send.at[d, number], recv.at[d, number],
+                source, landing.at[d], send.at[d, number], recv.at[d, number],
                 device_id={"seq": target}, device_id_type=MESH,
             )
             for number, (source, landing) in enumerate(pieces(target)) if number in numbers
@@ -114,7 +114,7 @@
 
     def own_copies(numbers=range(6)):
         return [
-            pltpu.make_async_copy(source, landing.at[me], local.at[number])
+            pltpu.make_async_copy(source, landing.at[0], local.at[number])
             for number, (source, landing) in enumerate(pieces(me)) if number in numbers
         ]
 
@@ -171,10 +171,12 @@
     source = section * 0
     for s in range(sections):
         source = jnp.where(owner[s] == section, s, source)
-    position = lax.broadcasted_iota(jnp.int32, bias.shape, 1)
-    bias[...] = jnp.where(position < counts[section], 0.0, MASKED)
-    position = lax.broadcasted_iota(jnp.int32, cbias.shape, 1)
-    cbias[...] = jnp.where(position < cap_len[source], 0.0, MASKED)
+    for ref, limit in ((bias, counts[section]), (cbias, cap_len[source])):
+        rows = ref.shape[1] // n
+        lanes = lax.broadcasted_iota(jnp.int32, ref.shape, 1)
+        step = me - lanes // rows
+        position = jnp.where(step < 0, step + n, step) * rows + lanes % rows
+        ref[...] = jnp.where(position < limit, 0.0, MASKED)
 
     @pl.loop(1, wides)
     def _(d):
@@ -185,44 +187,49 @@
         total = total + stats[w]
     factors[0:8] = lax.rsqrt(total / D + 1e-06)
     factor = factors[...].T
-    capr[section, 0] = scaled_rows(cap[0], factor[0:cap_rows, 3:4], gck[...])
-    k[...] = scaled_rows(k_raw[...], factor[:, 1:2], gk[...])
-    q[...] = scaled_rows(q_raw[...], factor[:, 0:1], gq[...])
-    cq[...] = scaled_rows(cq_raw[...], factor[:, 2:3], gcq[...])
+    capr[section, 0] = scaled_rows(cap[0], factor[0:cap_rows, 3:4], gck[...].reshape(1, -1))
+    k[...] = scaled_rows(k_raw[...], factor[:, 1:2], gk[...].reshape(1, -1))
+    q[...] = scaled_rows(q_raw[...], factor[:, 0:1], gq[...].reshape(1, -1))
+    cq[...] = scaled_rows(cq_raw[...], factor[:, 2:3], gcq[...].reshape(1, -1))
     for d in range(1, sections):
         to_section(d, 0).start()
-    start((0,))
-    start((2, 5))
+    start((5,))
+    start((2,))
     for d in range(1, sections):
         for number in range(2):
             to_section(d, number).wait_recv()
     chosen[...] = capr[source]
     start((3, 4))
-
-    def arrivals(d):
-        for number, landing in enumerate((kr, vr, qr, ckr, cvr, cqr)):
+    start((0,))
+
+    landings = (kr, vr, qr, ckr, cvr, cqr)
+
+    def arrived(d, numbers):
+        for number in numbers:
+            landing = landings[number].at[0]
             pltpu.make_async_remote_copy(
-                landing.at[0], landing.at[0], send.at[d, number], recv.at[d, number],
+                landing, landing, send.at[d, number], recv.at[d, number],
                 device_id={"seq": lax.rem(me + 1, n)}, device_id_type=MESH,
             ).wait_recv()
 
     columns = pl.ds(pl.multiple_of((mine // PER_HEAD) * HEAD, HEAD), HEAD)
 
-    def results(d, to, make):
+    def results(d, to, make, pairs=(0, 1)):
         rows = pl.ds(pl.multiple_of(third * STEP + EXTRA, 16), STEP)
         found = []
         for number, (buf, out) in enumerate(((os_buf, out_self), (oc_buf, out_cross))):
-            found.append(
-                make(buf.at[to, pl.ds(EXTRA, STEP)], out.at[rows, columns], d, 2 * number)
-            )
+            if number in pairs:
+                found.append(
+                    make(buf.at[to, pl.ds(EXTRA, STEP)], out.at[rows, columns], d, 2 * number)
+                )
         return found
 
-    def first_rows(d, to, make):
+    def first_rows(d, to, make, pairs=(0, 1)):
         found = []
         for number, (buf, out) in enumerate(((os_buf, out_self), (oc_buf, out_cross))):
-            found.append(
-                make(buf.at[to, pl.ds(0, EXTRA)], out.at[pl.ds(0, EXTRA), columns], d, 2 * number + 1)
-            )
+            if number in pairs:
+                landing = out.at[pl.ds(0, EXTRA), columns]
+                found.append(make(buf.at[to, pl.ds(0, EXTRA)], landing, d, 2 * number + 1))
         return found
 
     def remote(source, landing, d, number):
@@ -239,45 +246,78 @@
         for copy in own_copies():
             copy.wait()
 
+        def give(d, pairs):
+            back = lax.rem(n - d, n)
+            for near, make in ((True, nearby), (False, remote)):
+                @pl.when((d == 0) if near else (d > 0))
+                def _():
+                    for copy in results(back, d, make, pairs):
+                        copy.start()
+
+                    @pl.when(third == 0)
+                    def _():
+                        for copy in first_rows(back, d, make, pairs):
+                            copy.start()
+
+        def finish(buf, pairs, g):
+            buf[pl.ds(g * group, group)] = (accum[g] / total_w[g]).astype(
+                jnp.bfloat16
+            ).reshape(group, PIECE, HEAD)
+
+            @pl.when(g > 0)
+            def _():
+                give_group(g - 1, pairs)
+
+        def give_group(g, pairs):
+            @pl.loop(0, group)
+            def _(i):
+                give(g * group + i, pairs)
+
+        group = n // GROUPS
+        state = (top_w, total_w, accum)
+
         @pl.loop(1, n)
         def _(d):
-            arrivals(d)
-
-        group = 4
-
-        def give(g):
+            arrived(d, (2, 3, 4, 5))
+
+        @pl.loop(0, GROUPS)
+        def _(g):
+            queries[g] = cqr[pl.ds(g * group, group)].reshape(group * PIECE, HEAD)
+
+        first_state(state)
+        attend(
+            queries, ckr[...].reshape(-1, HEAD), cvr[...].reshape(-1, HEAD), cbias[0:1], state,
+            functools.partial(finish, oc_buf, (1,)),
+        )
+
+        @pl.loop(0, GROUPS)
+        def _(g):
+            queries[g] = qr[pl.ds(g * group, group)].reshape(group * PIECE, HEAD)
+
+        first_state(state)
+
+        give_group(GROUPS - 1, (1,))
+
+        def self_block(b, after):
             @pl.loop(0, group)
             def _(i):
-                to = g * group + i
-                d = lax.rem(to + n - me, n)
-                for near, make in ((True, nearby), (False, remote)):
-                    @pl.when((d == 0) if near else (d > 0))
-                    def _():
-                        for copy in results(d, to, make):
-                            copy.start()
-
-                        @pl.when(third == 0)
-                        def _():
-                            for copy in first_rows(d, to, make):
-                                copy.start()
-
-        @pl.loop(0, n // group)
-        def _(g):
-            queries = qr[pl.ds(g * group, group)].reshape(group * PIECE, HEAD)
-            os_buf[pl.ds(g * group, group)] = attend(queries, kr, vr, bias, 4).reshape(
-                group, PIECE, HEAD
+                @pl.when(b * group + i > 0)
+                def _():
+                    arrived(b * group + i, (1, 0))
+
+            slots = pl.ds(b * group, group)
+            block = group * kr.shape[1]
+            attend(
+                queries, kr[slots].reshape(block, HEAD), vr[slots].reshape(block, HEAD),
+                bias[0:1, pl.ds(pl.multiple_of(b * block, HEAD), block)], state, after,
             )
-            queries = cqr[pl.ds(g * group, group)].reshape(group * PIECE, HEAD)
-            oc_buf[pl.ds(g * group, group)] = attend(queries, ckr, cvr, cbias, 16).reshape(
-                group, PIECE, HEAD
-            )
-
-            @pl.when(g > 0)
-            def _():
-                give(g - 1)
-
-
-        give(n // group - 1)
+
+        @pl.loop(0, GROUPS - 1)
+        def _(b):
+            self_block(b, None)
+
+        self_block(GROUPS - 1, functools.partial(finish, os_buf, (0,)))
+        give_group(GROUPS - 1, (0,))
 
     @pl.loop(1, n)
     def _(d):
@@ -362,6 +402,10 @@
             pltpu.VMEM((8, rows), f32),
             pltpu.VMEM((wides, 8, rows), f32),
             pltpu.VMEM((HEAD, rows), f32),
+            pltpu.VMEM((GROUPS, n // GROUPS * PIECE, HEAD), bf16),
+            pltpu.VMEM((GROUPS, n // GROUPS * PIECE, HEAD), f32),
+            pltpu.VMEM((GROUPS, n // GROUPS * PIECE, HEAD), f32),
+            pltpu.VMEM((GROUPS, n // GROUPS * PIECE, HEAD), f32),
             dma((n, 6)), dma((n, 6)), dma((6,)),
             dma((n, 4)), dma((n, 4)), dma((4,)),
             dma((wides,)), dma((wides,)),
@@ -390,7 +434,7 @@
     out_self, out_cross = exchange_and_attend(
         counts, cap_len, owner,
         q_self[0], k_self[0], v_self[0], q_cross[0], cap_kv[:, 0],
-        gain_q_self[None], gain_k_self[None], gain_q_cross[None], gain_k_cross[None],
+        gain_q_self, gain_k_self, gain_q_cross, gain_k_cross,
     )
     return (out_self[None], out_cross[None])
 

time: 125 us -> 119 us (0.952)
  local copies, waits for them, and re-layouts: 5.72 us -> 2.5 us
  Pallas kernels: 118 us -> 115 us
    pallas_call x1, Pallas kernels: 118 us -> 115 us  [exchange_and_attend(): pl.pallas_call(functools.partial(main_kernel, n, sections, wides, width /...]
    broadcast_in_dim x4 -> x0, local copies, waits for them, and re-layouts: 2.33 us -> none  [the longest x1 0.59 us: per_device(): gain_k_cross[None]]
    unnamed x12 -> x4, local copies, waits for them, and re-layouts: 3.4 us -> 2.5 us
where the time goes in v4:
time: 119 us; the launch traced here: 118 us
  Pallas kernels  115 us (97%)
  local copies, waits for them, and re-layouts  2.5 us (2%)
    pallas_call x1, Pallas kernels, exchange_and_attend(): pl.pallas_call(functools.partial(main_kernel, n, sections, wides, width /...  115 us
    unnamed x4, local copies, waits for them, and re-layouts  2.5 us

profile of v4, /device:TPU:1, one launch (start us, length us, event | category | flops | bytes accessed | tf_op | source)
XLA Modules:
  0.0 117.7 jit_solution(12447409942714185363)
XLA Ops:
  0.6 114.6 %shard_map.131 = (bf16[256,640]{1,0:T(8,128)(2,1)}, bf16[256,640]{1,0:T(8,128)(2,1)}) custom-call(s32[4]{0:T(128)} %counts.1, s32[4]{0:T(128)} %cap_len.1, s32[4]{0:T(128)} %owner.1, bf16[256,640]{1,0:T(8,128)(2,1)} %bitcast.9, bf16[256,640]{1,0:T(8,128)(2,1)} %bitcast.10, bf16[256,640]{1,0:T(8,128)(2,1)} %bitcast.11, bf16[256,640]{1,0:T(8,128)(2,1)} %bitcast.12, ...), custom_call_target="tpu_custom_call" | custom-call | tf_op jit(solution)/shard_map/pallas_call | solution.py:377
  115.2 0.0 copy-start
  115.2 1.8 %copy.16 = bf16[1,256,640]{2,1,0:T(8,128)(2,1)} copy(bf16[1,256,640]{2,1,0:T(8,128)(2,1)} %bitcast.8) | data formatting | bytes 655360
  117.0 0.0 copy-done
  117.0 0.7 copy.17
Async XLA Ops:
  115.2 1.8 %copy-start = (bf16[256,640]{1,0:T(8,128)(2,1)S(1)}, bf16[256,640]{1,0:T(8,128)(2,1)}, u32[]{:S(2)}) copy-start(bf16[256,640]{1,0:T(8,128)(2,1)} %get-tuple-element.5) | copy-start | bytes 983044
